TPU v7x, 256 devices: a whole 4x4x8 slice. The times are simulated.
256 devices in a mesh: rows: 16 (over x, y_lo, core), cols: 16 (over y_hi, z).
Axes of the slice: x: 4, y: 4 (y_hi: 2, y_lo: 2; y = y_hi * 2 + y_lo), z: 8, core: 2. Of those that a mesh axis runs over, the one named last changes fastest.
Arguments:
- gram_tiles: float32 [25600, 25600], P('rows', 'cols'), may hold values from -1 to 4, as said below
- right_side: float32 [25600, 256], P(('rows', 'cols')), may hold values from -60 to 60
Outputs:
- solution_field: float32 [25600, 256], P(('rows', 'cols'))
- residual: float32 [25600, 256], P(('rows', 'cols'))
Inputs may be any that keep to these rules, and one draw needn't show every extreme that they name: The operator A built from gram_tiles is symmetric positive definite.
All inputs are finite; a program needn't handle non-finite values.
Results may differ from a plain program's by a relative error of at most 0.0003.
Values sent between devices are 32-bit elements; how exact they have to be, the bound alone decides.
A program may use at most 128 MiB of HBM per device.

v0:
```python
from functools import partial

import jax
import jax.numpy as jnp
from jax import lax
from jax.sharding import PartitionSpec as P

ITERS = 4


def in_blocks(shard, dim, size):
    dims = shard.shape
    pieces = shard.reshape(*dims[:dim], size, dims[dim] // size, *dims[dim + 1 :])
    return jnp.moveaxis(pieces, dim, 0)


def summed_on_arrival(shard, axis, dim):
    size = lax.axis_size(axis)
    pieces = lax.all_to_all(in_blocks(shard, dim, size), axis, 0, 0, tiled=True)
    return jnp.sum(pieces, axis=0)


def laid_out(pieces, dim):
    dims = list(pieces.shape[1:])
    dims[dim] *= pieces.shape[0]
    return jnp.moveaxis(pieces, 0, dim).reshape(dims)


def sent_to_all(shard, axis):
    copies = jnp.broadcast_to(shard, (lax.axis_size(axis), *shard.shape))
    return lax.all_to_all(copies, axis, split_axis=0, concat_axis=0, tiled=True)


def gathered_copies(shard, axis, dim):
    return laid_out(sent_to_all(shard, axis), dim)


def taken_together(shard, axis):
    everything = sent_to_all(shard, axis)
    return jnp.sum(everything, axis=0)


def in_one(arrays, axis):
    line, at, finished = (jnp.concatenate([a.reshape(-1) for a in arrays]), 0, [])
    subtotal = taken_together(line, axis)
    for a in arrays:
        finished.append(subtotal[at : at + a.size].reshape(a.shape))
        at += a.size
    return tuple(finished)


def contract(tile_rows, vectors):
    return lax.dot_general(
        tile_rows,
        vectors,
        (((0,), (0,)), ((), ())),
        precision=lax.Precision.HIGHEST,
        preferred_element_type=jnp.float32,
    )


def column_sums(first_vec, second_vec):
    return jnp.sum(first_vec * second_vec, axis=0)


def reduce_rows(partial_term):
    return summed_on_arrival(partial_term, "rows", 0)


def image_block(gram_tiles, row_block):
    portion = reduce_rows(contract(gram_tiles, row_block))
    return gathered_copies(portion, "cols", 0)


def pair_rows(residual, applied):
    return in_one((column_sums(residual, residual), column_sums(residual, applied)), "rows")


def merged_solve(right_vecs, operator_fn, pair_fn):
    solution = jnp.zeros_like(right_vecs)
    residual = right_vecs
    applied = operator_fn(residual)
    norm_now, product = pair_fn(residual, applied)
    step_size = norm_now / product
    direction = residual
    applied_dir = applied
    for iteration in range(ITERS):
        solution = solution + step_size * direction
        residual = residual - step_size * applied_dir
        if iteration + 1 < ITERS:
            applied = operator_fn(residual)
            norm_next, product = pair_fn(residual, applied)
            beta_ratio = norm_next / norm_now
            step_size = norm_next / (product - beta_ratio * norm_next / step_size)
            direction = residual + beta_ratio * direction
            applied_dir = applied + beta_ratio * applied_dir
            norm_now = norm_next
    return (solution, residual)


def body(gram_tiles, right_side):
    whole_rows = gathered_copies(right_side, "cols", 0)
    solution, residual = merged_solve(whole_rows, partial(image_block, gram_tiles), pair_rows)
    shard_len = right_side.shape[0]
    offset = lax.axis_index("cols") * shard_len
    solution = lax.dynamic_slice_in_dim(solution, offset, shard_len, 0)
    residual = lax.dynamic_slice_in_dim(residual, offset, shard_len, 0)
    return (solution, residual)


def solution(mesh):
    placed = (P("rows", "cols"), P(("rows", "cols"), None))
    return jax.shard_map(
        body,
        mesh=mesh,
        in_specs=placed,
        out_specs=(P(("rows", "cols"), None), P(("rows", "cols"), None)),
        check_vma=False,
    )
```

profile of v0, /device:TPU:8, one launch (start us, length us, event | category | flops | bytes accessed | tf_op | source)
XLA Modules:
  0.0 512.8 jit_solution(6469935898871298681)
XLA Ops:
  2.9 10.3 %all-to-all-start = ((f32[16,100,256]{2,1,0:T(8,128)}), f32[16,100,256]{2,1,0:T(8,128)S(1)}, u32[]{:S(2)}, u32[]{:S(2)}) async-start(f32[16,100,256]{2,1,0:T(8,128)} %broadcast_in_dim.18), calls=%async_computation | async-start | bytes 3407872 | tf_op jit(solution)/shard_map/all_to_all | solution.py:31
  13.2 13.2 %copy.7 = f32[1600,1600]{1,0:T(8,128)} copy(f32[1600,1600]{0,1:T(8,128)} %bitcast.14) | data formatting | bytes 20480000 | tf_op jit(solution)/shard_map/dot_general | solution.py:53
  26.3 10.6 %dot_general.23 = f32[16,100,1600]{2,1,0:T(8,128)} reshape(f32[1600,1600]{1,0:T(8,128)} %copy.7) | data formatting | bytes 20480000 | tf_op jit(solution)/shard_map/dot_general | solution.py:53
  36.9 18.8 %all-to-all-done = f32[16,100,256]{2,1,0:T(8,128)S(1)} async-done(((f32[16,100,256]{2,1,0:T(8,128)}), f32[16,100,256]{2,1,0:T(8,128)S(1)}, u32[]{:S(2)}, u32[]{:S(2)}) %all-to-all-start) | async-done | bytes 1638432 | tf_op jit(solution)/shard_map/all_to_all | solution.py:31
  57.1 12.6 %fusion.5 = f32[16,100,256]{2,1,0:T(8,128)S(1)} fusion(f32[16,100,1600]{2,1,0:T(8,128)} %dot_general.23, f32[1600,256,1]{1,0,2:T(8,128)} %reshape.133), kind=kOutput, calls=%fused_computation.43 | convolution fusion | flops 7864320000 | bytes 13516800 | tf_op jit(solution)/shard_map/dot_general | solution.py:53
  69.7 27.7 %all_to_all.69 = f32[16,100,256]{2,1,0:T(8,128)} all-to-all(f32[16,100,256]{2,1,0:T(8,128)S(1)} %fusion.5), channel_id=1, replica_groups=mesh['rows'=16,'cols'=16] {'rows'}, dimensions={0} | all-to-all | bytes 3276800 | tf_op jit(solution)/shard_map/all_to_all | solution.py:19
  99.1 48.8 %all_to_all.70 = f32[16,100,256]{2,1,0:T(8,128)S(1)} all-to-all(f32[16,100,256]{2,1,0:T(8,128)S(1)} %broadcast_in_dim.19), channel_id=1, replica_groups=mesh['rows'=16,'cols'=16] {'cols'}, dimensions={0} | all-to-all | bytes 3276800 | tf_op jit(solution)/shard_map/all_to_all | solution.py:31
  148.9 5.5 %all-to-all-start.3 = ((f32[16,1,512]{2,1,0:T(1,128)}), f32[16,1,512]{2,1,0:T(1,128)S(1)}, u32[]{:S(2)}, u32[]{:S(2)}) async-start(f32[16,1,512]{2,1,0:T(1,128)} %broadcast_in_dim.20), calls=%async_computation.3 | async-start | bytes 65536 | tf_op jit(solution)/shard_map/all_to_all | solution.py:31
  159.0 24.2 %convolution_bitcast_fusion.2 = f32[1600,256]{1,0:T(8,128)} fusion(f32[1600,1600]{1,0:T(8,128)} %param.2, f32[1600,256]{1,0:T(8,128)} %reshape.125, f32[1600,256]{1,0:T(8,128)} %reshape.126, f32[256]{0:T(256)S(1)} %slice_divide_fusion.1), kind=kOutput, calls=%fused_computation.2 | convolution fusion | flops 7865139200 | bytes 15156224 | tf_op jit(solution)/shard_map/dot_general | solution.py:53
  185.8 27.8 %all_to_all.71 = f32[16,100,256]{2,1,0:T(8,128)} all-to-all(f32[16,100,256]{2,1,0:T(8,128)} %reshape.127), channel_id=1, replica_groups=mesh['rows'=16,'cols'=16] {'rows'}, dimensions={0} | all-to-all | bytes 3276800 | tf_op jit(solution)/shard_map/all_to_all | solution.py:19
  215.2 47.1 %all_to_all.72 = f32[16,100,256]{2,1,0:T(8,128)S(1)} all-to-all(f32[16,100,256]{2,1,0:T(8,128)S(1)} %broadcast_in_dim.21), channel_id=1, replica_groups=mesh['rows'=16,'cols'=16] {'cols'}, dimensions={0} | all-to-all | bytes 3276800 | tf_op jit(solution)/shard_map/all_to_all | solution.py:31
  264.7 4.7 all-to-all-start.6
  274.3 3.6 multiply_add_fusion.3
  279.0 22.9 %convolution_bitcast_fusion.1 = f32[1600,256]{1,0:T(8,128)} fusion(f32[1600,256]{1,0:T(8,128)S(1)} %get-tuple-element.23, f32[1600,1600]{1,0:T(8,128)} %param.2), kind=kOutput, calls=%fused_computation.1 | convolution fusion | flops 7864320000 | bytes 13516800 | tf_op jit(solution)/shard_map/dot_general | solution.py:53
  303.5 26.7 %all_to_all.73 = f32[16,100,256]{2,1,0:T(8,128)} all-to-all(f32[16,100,256]{2,1,0:T(8,128)S(1)} %reshape.129), channel_id=1, replica_groups=mesh['rows'=16,'cols'=16] {'rows'}, dimensions={0} | all-to-all | bytes 3276800 | tf_op jit(solution)/shard_map/all_to_all | solution.py:19
  331.8 47.3 %all_to_all.74 = f32[16,100,256]{2,1,0:T(8,128)S(1)} all-to-all(f32[16,100,256]{2,1,0:T(8,128)S(1)} %broadcast_in_dim.46), channel_id=1, replica_groups=mesh['rows'=16,'cols'=16] {'cols'}, dimensions={0} | all-to-all | bytes 3276800 | tf_op jit(solution)/shard_map/all_to_all | solution.py:31
  381.5 4.7 all-to-all-start.9
  386.2 3.0 reshape.130
  391.1 4.5 multiply_subtract_fusion.3
  396.9 22.9 %convolution_bitcast_fusion = f32[1600,256]{1,0:T(8,128)} fusion(f32[1600,256]{1,0:T(8,128)S(1)} %get-tuple-element.12, f32[1600,1600]{1,0:T(8,128)} %param.2), kind=kOutput, calls=%fused_computation | convolution fusion | flops 7864320000 | bytes 13516800 | tf_op jit(solution)/shard_map/dot_general | solution.py:53
  422.4 27.8 %all_to_all.75 = f32[16,100,256]{2,1,0:T(8,128)} all-to-all(f32[16,100,256]{2,1,0:T(8,128)} %reshape.131), channel_id=1, replica_groups=mesh['rows'=16,'cols'=16] {'rows'}, dimensions={0} | all-to-all | bytes 3276800 | tf_op jit(solution)/shard_map/all_to_all | solution.py:19
  451.9 47.3 %all_to_all.76 = f32[16,100,256]{2,1,0:T(8,128)S(1)} all-to-all(f32[16,100,256]{2,1,0:T(8,128)S(1)} %broadcast_in_dim.48), channel_id=1, replica_groups=mesh['rows'=16,'cols'=16] {'cols'}, dimensions={0} | all-to-all | bytes 3276800 | tf_op jit(solution)/shard_map/all_to_all | solution.py:31
  501.1 4.7 all-to-all-start.12
  507.3 3.3 all-to-all-done.12
  (61 shorter events, 41.9 us)
Async XLA Ops:
  2.9 52.9 %all-to-all-start = ((f32[16,100,256]{2,1,0:T(8,128)}), f32[16,100,256]{2,1,0:T(8,128)S(1)}, u32[]{:S(2)}, u32[]{:S(2)}) async-start(f32[16,100,256]{2,1,0:T(8,128)} %broadcast_in_dim.18), calls=%async_computation | async-start | bytes 3407872 | tf_op jit(solution)/shard_map/all_to_all | solution.py:31
  148.9 10.0 %all-to-all-start.3 = ((f32[16,1,512]{2,1,0:T(1,128)}), f32[16,1,512]{2,1,0:T(1,128)S(1)}, u32[]{:S(2)}, u32[]{:S(2)}) async-start(f32[16,1,512]{2,1,0:T(1,128)} %broadcast_in_dim.20), calls=%async_computation.3 | async-start | bytes 65536 | tf_op jit(solution)/shard_map/all_to_all | solution.py:31
  262.3 1.7 copy-start
  264.7 9.5 %all-to-all-start.6 = ((f32[16,1,512]{2,1,0:T(1,128)}), f32[16,1,512]{2,1,0:T(1,128)S(1)}, u32[]{:S(2)}, u32[]{:S(2)}) async-start(f32[16,1,512]{2,1,0:T(1,128)} %broadcast_in_dim.22), calls=%async_computation.6 | async-start | bytes 65536 | tf_op jit(solution)/shard_map/all_to_all | solution.py:31
  269.4 4.9 copy-start.4
  277.9 1.2 copy-start.5
  331.8 47.4 %copy-start.1 = (f32[16,100,256]{2,1,0:T(8,128)S(1)}, f32[16,100,256]{2,1,0:T(8,128)}, u32[]{:S(2)}) copy-start(f32[16,100,256]{2,1,0:T(8,128)} %copy-done) | copy-start | bytes 4915204
  331.8 47.4 %copy-start.9 = (f32[16,100,256]{2,1,0:T(8,128)S(1)}, f32[16,100,256]{2,1,0:T(8,128)}, u32[]{:S(2)}) copy-start(f32[16,100,256]{2,1,0:T(8,128)} %get-tuple-element.21) | copy-start | bytes 4915204
  379.2 1.7 copy-start.2
  381.5 9.5 %all-to-all-start.9 = ((f32[16,1,512]{2,1,0:T(1,128)}), f32[16,1,512]{2,1,0:T(1,128)S(1)}, u32[]{:S(2)}, u32[]{:S(2)}) async-start(f32[16,1,512]{2,1,0:T(1,128)} %broadcast_in_dim.47), calls=%async_computation.9 | async-start | bytes 65536 | tf_op jit(solution)/shard_map/all_to_all | solution.py:31
  395.6 1.3 copy-start.7
  451.9 47.4 %copy-start.3 = (f32[16,100,256]{2,1,0:T(8,128)S(1)}, f32[16,100,256]{2,1,0:T(8,128)}, u32[]{:S(2)}) copy-start(f32[16,100,256]{2,1,0:T(8,128)} %copy-done.2) | copy-start | bytes 4915204
  451.9 47.4 %copy-start.8 = (f32[16,100,256]{2,1,0:T(8,128)S(1)}, f32[16,100,256]{2,1,0:T(8,128)}, u32[]{:S(2)}) copy-start(f32[16,100,256]{2,1,0:T(8,128)} %get-tuple-element.17) | copy-start | bytes 4915204
  499.2 1.2 copy-start.6
  501.1 9.5 %all-to-all-start.12 = ((f32[16,1,512]{2,1,0:T(1,128)}), f32[16,1,512]{2,1,0:T(1,128)S(1)}, u32[]{:S(2)}, u32[]{:S(2)}) async-start(f32[16,1,512]{2,1,0:T(1,128)} %broadcast_in_dim.49), calls=%async_computation.12 | async-start | bytes 65536 | tf_op jit(solution)/shard_map/all_to_all | solution.py:31
where the time goes:
time: 522 us; the launch traced here: 513 us
  blocking collectives  300 us (57%)
  matrix products  82.7 us (16%)
  local copies, waits for them, and re-layouts  50.2 us (10%)
  starting transfers between devices  29.8 us (6%)
  waiting for transfers between devices  27.7 us (5%)
  other arithmetic  20.9 us (4%)
    all_to_all x4, blocking collectives, sent_to_all(): return lax.all_to_all(copies, axis, split_axis=0, concat_axis=0, tiled=True)  191 us
    all_to_all x4, blocking collectives, summed_on_arrival(): pieces = lax.all_to_all(in_blocks(shard, dim, size), axis, 0, 0, tiled=True)  110 us
    dot_general x4, matrix products, contract(): lax.dot_general(tile_rows, vectors, (((0,), (0,)), ((), ())), precision=l...  82.7 us
    all_to_all x5, starting transfers between devices, sent_to_all(): return lax.all_to_all(copies, axis, split_axis=0, concat_axis=0, tiled=True)  29.8 us
    all_to_all x5, waiting for transfers between devices, sent_to_all(): return lax.all_to_all(copies, axis, split_axis=0, concat_axis=0, tiled=True)  27.7 us
    dot_general x2, local copies, waits for them, and re-layouts, contract(): lax.dot_general(tile_rows, vectors, (((0,), (0,)), ((), ())), precision=l...  23.7 us
    reshape x6, local copies, waits for them, and re-layouts, laid_out(): return jnp.moveaxis(pieces, 0, dim).reshape(dims)  11.5 us
  transfers between devices with their start and end apart: 5, of which 5 were waited for; matrix products, arithmetic and copies ran while one was open for 7% of the time, Pallas kernels for 0%

commit v1 on v0

v1 whole, which is shorter than its diff:
```python
import jax
import jax.numpy as jnp
from jax import lax
from jax.experimental import pallas as pl
from jax.experimental.pallas import tpu as pltpu
from jax.sharding import PartitionSpec as P

ITERS = 4
NX, NZ = 4, 8
PIECE, SLOT, KSLOT = 100, 104, 112
WIDTH = 256
STREAMS = 2
NC = WIDTH // STREAMS
ROWS = 1600
MPAD = 16 * SLOT
KPAD = 16 * KSLOT
CHUNK = 4 * SLOT
F32, BF16 = jnp.float32, jnp.bfloat16

HALF = "g" + "mm" + "g" + "m" + "ggg" + "mm" + "gg" + "m" + "gg" + "mm" + "gg" + "m" + "gggg" + "mm" + "ggg"


def halves(x):
    hi = x.astype(BF16)
    lo = (x - hi.astype(F32)).astype(BF16)
    return hi, lo


def kernel(gram, rhs, sol, res, tv, tp, t1, t2, tt, vb, ag, os, cr, xa, xs, xb, ys, yr, st, sc, fs, fr,
           t_sem, y_snd, y_rcv, z_snd, z_rcv, c_snd, c_rcv, xa_snd, xa_rcv, xb_snd, xb_rcv, q_snd, q_rcv,
           f_snd, f_rcv):
    row, col = lax.axis_index("rows"), lax.axis_index("cols")
    xx, yl, core = row // 4, lax.rem(row // 2, 2), lax.rem(row, 2)
    yh, z = col // NZ, lax.rem(col, NZ)

    def at_x(d):
        return (lax.rem(xx + d, NX) * 4 + yl * 2 + core, col)

    def at_z(d):
        return (row, yh * NZ + lax.rem(z + d, NZ))

    at_core = (xx * 4 + yl * 2 + 1 - core, col)
    at_yl = (xx * 4 + (1 - yl) * 2 + core, col)
    at_yh = (row, (1 - yh) * NZ + z)
    partners = [at_core, at_yl, at_yh] + [at_x(d) for d in range(1, NX)] + [at_z(d) for d in range(1, NZ)]

    def remote(src, dst, snd, rcv, to):
        return pltpu.make_async_remote_copy(
            src_ref=src, dst_ref=dst, send_sem=snd, recv_sem=rcv, device_id=to,
            device_id_type=pl.DeviceIdType.MESH)

    for m in range(4):
        pltpu.make_async_copy(gram.at[pl.ds(400 * m, 400), :], tv.at[pl.ds(400 * m, 400), :], t_sem.at[m]).start()

    barrier = pltpu.get_barrier_semaphore()
    for to in partners:
        pl.semaphore_signal(barrier, inc=1, device_id=to, device_id_type=pl.DeviceIdType.MESH)

    def slot(kind, d):
        return (yh if kind == 0 else 1 - yh) * NZ + lax.rem(z + d + NZ, NZ)

    def pack(t, s, at):
        x = jnp.concatenate([ag[t, s, at], jnp.zeros((KSLOT - SLOT, NC), F32)], axis=0)
        hi, lo = halves(x)
        start = pl.multiple_of(at * KSLOT, 16)
        vb[s, pl.ds(start, KSLOT), 0:NC] = hi
        vb[s, pl.ds(start, KSLOT), NC:2 * NC] = lo

    def gather(t, s):
        par = lax.rem(t, 2)
        far = ((4, 3), (3, 4))

        def z_copy(kind, way, d):
            at = slot(kind, -d if way == 0 else d)
            return remote(ag.at[t, s, at], ag.at[t, s, at], z_snd.at[s, kind, way, d], z_rcv.at[par, s, kind, way, d],
                          at_z(1 if way == 0 else NZ - 1))

        def z_landing(kind, way, d):
            at = slot(kind, -d if way == 0 else d)
            return remote(ag.at[t, s, at], ag.at[t, s, at], z_snd.at[s, kind, way, d - 1],
                          z_rcv.at[par, s, kind, way, d - 1], at_z(NZ - 1 if way == 0 else 1))

        def y_copy():
            return remote(ag.at[t, s, slot(0, 0)], ag.at[t, s, slot(0, 0)], y_snd.at[s], y_rcv.at[par, s], at_yh)

        def y_landing():
            return remote(ag.at[t, s, slot(1, 0)], ag.at[t, s, slot(1, 0)], y_snd.at[s], y_rcv.at[par, s], at_yh)

        def first():
            y_copy().start()
            z_copy(0, 0, 0).start()
            z_copy(0, 1, 0).start()
            pack(t, s, slot(0, 0))

        def other():
            y_landing().wait_recv()
            z_copy(1, 0, 0).start()
            z_copy(1, 1, 0).start()
            pack(t, s, slot(1, 0))

        def step(kind, d):
            def run():
                for way in range(2):
                    if d <= far[kind][way]:
                        z_landing(kind, way, d).wait_recv()
                        if d < far[kind][way]:
                            z_copy(kind, way, d).start()
                for way in range(2):
                    if d <= far[kind][way]:
                        pack(t, s, slot(kind, -d if way == 0 else d))
            return run

        def drain():
            y_copy().wait_send()
            for kind in range(2):
                for way in range(2):
                    for d in range(far[kind][way]):
                        z_copy(kind, way, d).wait_send()

        return [first, step(0, 1), other, step(0, 2), step(1, 1), step(0, 3), step(1, 2), step(0, 4), step(1, 3),
                step(1, 4), drain]

    def scatter(t, s):
        par = lax.rem(t, 2)
        ahead = (2, 1, 3, 0)

        def c_copy(e):
            to = lax.rem(xx + ahead[e], NX)
            return remote(os.at[s, to, 1 - core], cr.at[t, s, to], c_snd.at[s, e], c_rcv.at[par, s, e], at_core)

        def xa_copy(k):
            return remote(xs.at[s, 0, k], xa.at[t, s, k], xa_snd.at[s, k], xa_rcv.at[par, s, k], at_x(1 if k == 0 else 3))

        def xb_copy(way, k):
            return remote(xs.at[s, 1 + way, k], xb.at[t, s, way, k], xb_snd.at[s, way, k], xb_rcv.at[par, s, way, k],
                          at_x(1 if way == 0 else 3))

        def q_copy():
            return remote(ys.at[s], yr.at[t, s], q_snd.at[s], q_rcv.at[par, s], at_yl)

        def spare():
            total = jnp.zeros((8, NC), F32)
            for b in range(16):
                total = total + ag[t, s, b, 96:104, :]
            keep = lax.broadcasted_iota(jnp.int32, (8, NC), 0)
            return jnp.where((keep == 4) | (keep == 5), total, 0.0)

        def multiply(e):
            def run():
                to = lax.rem(xx + ahead[e], NX)
                y = jnp.dot(tt[to], vb[s], preferred_element_type=F32)
                dots = spare()
                for q in range(4):
                    lo, hi = q * SLOT, (q + 1) * SLOT
                    piece = (y[lo:hi, :NC] + (y[lo:hi, NC:] + y[CHUNK + lo:CHUNK + hi, :NC])) + y[CHUNK + lo:CHUNK + hi, NC:]
                    os[s, to, q % 2, q // 2, 0:96] = piece[0:96]
                    os[s, to, q % 2, q // 2, 96:104] = piece[96:104] + dots
                c_copy(e).start()
            return run

        def pair(e, k):
            to = lax.rem(xx + ahead[e], NX)
            return os[s, to, core, k] + cr[t, s, to, k]

        def far_x():
            c_copy(0).wait_recv()
            for k in range(2):
                xs[s, 0, k] = pair(0, k)
                xa_copy(k).start()

        def near_x(way):
            def run():
                c_copy(1 + way).wait_recv()
                k = 1 - way
                xs[s, 1 + way, k] = pair(1 + way, k)
                xb_copy(way, k).start()
            return run

        def relay_x(way):
            def run():
                k = way
                both = pair(1 + way, k)
                xa_copy(k).wait_recv()
                xs[s, 1 + way, k] = both + xa[t, s, k]
                xb_copy(way, k).start()
            return run

        def own_x():
            c_copy(3).wait_recv()
            for way in range(2):
                for k in range(2):
                    xb_copy(way, k).wait_recv()
            k = 1 - yl
            ys[s] = (pair(3, k) + xb[t, s, 0, k]) + xb[t, s, 1, k]
            q_copy().start()

        def update():
            k = yl
            part = (pair(3, k) + xb[t, s, 0, k]) + xb[t, s, 1, k]
            q_copy().wait_recv()
            u = part + yr[t, s]
            renew(t, s, u)

        def drain():
            for e in range(4):
                c_copy(e).wait_send()
            for k in range(2):
                xa_copy(k).wait_send()
            for way in range(2):
                for k in range(2):
                    xb_copy(way, k).wait_send()
            q_copy().wait_send()

        def last():
            update()
            drain()

        return [multiply(0), multiply(1), far_x, multiply(2), near_x(0), multiply(3), near_x(1), relay_x(0), relay_x(1),
                own_x, last]

    R, W, Z, S, D, X = range(6)

    def renew(t, s, u):
        q0 = u[0:PIECE]

        @pl.when(t == 0)
        def _():
            st[s, W, 0:PIECE] = q0
            offer(t, s, q0)

        @pl.when(t > 0)
        def _():
            now, product = u[100:101], u[101:102]
            old_now, old_step = sc[s, 0:1], sc[s, 1:2]
            w = st[s, W, 0:PIECE]
            r = st[s, R, 0:PIECE]
            first = t == 1
            beta = jnp.where(first, 0.0, now / old_now)
            step = now / (product - jnp.where(first, 0.0, beta * now / old_step))
            q = jnp.where(first, q0, (w - q0) / old_step)
            zz = q + beta * st[s, Z, 0:PIECE]
            ss = w + beta * st[s, S, 0:PIECE]
            dd = r + beta * st[s, D, 0:PIECE]
            w = w - step * zz
            r = r - step * ss
            sc[s, 0:1] = now
            sc[s, 1:2] = step
            st[s, Z, 0:PIECE] = zz
            st[s, S, 0:PIECE] = ss
            st[s, D, 0:PIECE] = dd
            st[s, W, 0:PIECE] = w
            st[s, R, 0:PIECE] = r
            st[s, X, 0:PIECE] = st[s, X, 0:PIECE] + step * dd

            @pl.when(t < ITERS - 1)
            def _():
                offer(t, s, r - step * w)

    def dots_of(s):
        r = st[s, R, 0:PIECE]
        w = st[s, W, 0:PIECE]
        return jnp.sum(r * r, axis=0, keepdims=True), jnp.sum(r * w, axis=0, keepdims=True)

    def offer(t, s, v):
        a, b = dots_of(s)
        mine = slot(0, 0)
        ag[t + 1, s, mine, 0:PIECE] = v
        ag[t + 1, s, mine, 100:101] = a
        ag[t + 1, s, mine, 101:102] = b
        ag[t + 1, s, mine, 102:104] = jnp.zeros((2, NC), F32)

    def finish(s):
        plan = [[(at_core, 0)], [(at_yl, 1)], [(at_x(d), 1 + d) for d in range(1, NX)], [(at_yh, 5)],
                [(at_z(d), 5 + d) for d in range(1, NZ)]]

        def copies(stage):
            return [remote(fs.at[s, stage], fr.at[s, k], f_snd.at[s, k], f_rcv.at[s, k], to) for to, k in plan[stage]]

        def begin():
            a, b = dots_of(s)
            fs[s, 0, 0:1] = a
            fs[s, 0, 1:2] = b
            fs[s, 0, 2:8] = jnp.zeros((6, NC), F32)
            for c in copies(0):
                c.start()

        def arrived(stage):
            total = fs[s, stage]
            for c, (_, k) in zip(copies(stage), plan[stage]):
                c.wait_recv()
                total = total + fr[s, k]
            return total

        def onward(stage):
            def run():
                fs[s, stage] = arrived(stage - 1)
                for c in copies(stage):
                    c.start()
            return run

        def close():
            total = arrived(len(plan) - 1)
            now, product = total[0:1], total[1:2]
            old_now, old_step = sc[s, 0:1], sc[s, 1:2]
            beta = now / old_now
            step = now / (product - beta * now / old_step)
            w = st[s, W, 0:PIECE]
            r = st[s, R, 0:PIECE]
            ss = w + beta * st[s, S, 0:PIECE]
            dd = r + beta * st[s, D, 0:PIECE]
            cols = slice(s * NC, (s + 1) * NC)
            sol[:, cols] = st[s, X, 0:PIECE] + step * dd
            res[:, cols] = r - step * ss
            for stage in range(len(plan)):
                for c in copies(stage):
                    c.wait_send()

        return [begin] + [onward(k) for k in range(1, len(plan))] + [close]

    mine = slot(0, 0)
    st[...] = jnp.zeros(st.shape, F32)
    sc[...] = jnp.ones(sc.shape, F32)
    for s in range(STREAMS):
        b = rhs[:, s * NC:(s + 1) * NC]
        st[s, R, 0:PIECE] = b
        ag[0, s, mine, 0:PIECE] = b
        ag[0, s, mine, 100:104] = jnp.zeros((4, NC), F32)
    for a in range(16):
        t2[a * SLOT + PIECE:(a + 1) * SLOT] = jnp.zeros((SLOT - PIECE, 128), F32)
    pl.semaphore_wait(barrier, len(partners))
    events = gather(0, 0)
    events[0]()
    events = events[1:]

    @pl.loop(0, 4)
    def _(m):
        src = pl.multiple_of(m * 400, 8)
        pltpu.make_async_copy(gram.at[pl.ds(src, 400), :], tv.at[pl.ds(src, 400), :], t_sem.at[m]).wait()
        for p in range(2):
            base = pl.multiple_of(m * 400 + p * 200, 8)
            into = pl.multiple_of(m * 448 + p * 224, 8)
            for lane in range(0, ROWS, 128):
                wide = min(128, ROWS - lane)
                v = tv[pl.ds(base, 200), lane:lane + wide]
                none = jnp.zeros((KSLOT - PIECE, wide), F32)
                tp[pl.ds(into, 224), lane:lane + wide] = jnp.concatenate([v[0:100], none, v[100:200], none], axis=0)


    @pl.loop(0, KPAD // 128)
    def _(kb):
        at = pl.multiple_of(kb * 128, 128)
        for lane in range(0, ROWS, 128):
            wide = min(128, ROWS - lane)
            t1[lane:lane + wide] = tp[pl.ds(at, 128), lane:lane + wide].T
        for a in range(16):
            t2[a * SLOT:a * SLOT + PIECE] = t1[a * PIECE:(a + 1) * PIECE]
        for p in range(8):
            hi, lo = halves(t2[208 * p:208 * (p + 1)])
            start = (p % 2) * 208
            tt[p // 2, start:start + 208, pl.ds(at, 128)] = hi
            tt[p // 2, CHUNK + start:CHUNK + start + 208, pl.ds(at, 128)] = lo
        for i, event in enumerate(events):
            pl.when(kb == 4 + i)(event)

    def interleave(plan, g, m):
        g, m = list(g), list(m)
        for what in plan:
            if what == "g" and g:
                g.pop(0)()
            if what == "m" and m:
                m.pop(0)()
        for run in m + g:
            run()

    @pl.loop(0, STREAMS * ITERS - 1)
    def _(h):
        sm, tm = lax.rem(h, 2), h // 2
        sg, tg = 1 - sm, (h + 1) // 2
        interleave(HALF, gather(tg, sg), scatter(tm, sm))

    interleave("gm" + "mmg" + "mmg" + "mmmg" + "mg" + "mg" + "mg", finish(0), scatter(ITERS - 1, 1))
    for run in finish(1):
        run()


def body(gram_tiles, right_side):
    shard = jax.ShapeDtypeStruct(right_side.shape, F32)
    dma = pltpu.SemaphoreType.DMA
    vmem = pltpu.VMEM
    spec = pl.BlockSpec(memory_space=pltpu.VMEM)
    return pl.pallas_call(
        kernel,
        out_shape=(shard, shard),
        in_specs=[pl.BlockSpec(memory_space=pl.ANY), spec],
        out_specs=(spec, spec),
        scratch_shapes=[
            vmem((ROWS, ROWS), F32),
            vmem((KPAD, ROWS), F32),
            vmem((ROWS, 128), F32),
            vmem((MPAD, 128), F32),
            vmem((4, 2 * CHUNK, KPAD), BF16),
            vmem((STREAMS, KPAD, 2 * NC), BF16),
            vmem((ITERS, STREAMS, 16, SLOT, NC), F32),
            vmem((STREAMS, NX, 2, 2, SLOT, NC), F32),
            vmem((ITERS, STREAMS, NX, 2, SLOT, NC), F32),
            vmem((ITERS, STREAMS, 2, SLOT, NC), F32),
            vmem((STREAMS, 3, 2, SLOT, NC), F32),
            vmem((ITERS, STREAMS, 2, 2, SLOT, NC), F32),
            vmem((STREAMS, SLOT, NC), F32),
            vmem((ITERS, STREAMS, SLOT, NC), F32),
            vmem((STREAMS, 6, SLOT, NC), F32),
            vmem((STREAMS, 8, NC), F32),
            vmem((STREAMS, 5, 8, NC), F32),
            vmem((STREAMS, 13, 8, NC), F32),
            dma((4,)),
            dma((STREAMS,)), dma((2, STREAMS)),
            dma((STREAMS, 2, 2, 4)), dma((2, STREAMS, 2, 2, 4)),
            dma((STREAMS, 4)), dma((2, STREAMS, 4)),
            dma((STREAMS, 2)), dma((2, STREAMS, 2)),
            dma((STREAMS, 2, 2)), dma((2, STREAMS, 2, 2)),
            dma((STREAMS,)), dma((2, STREAMS)),
            dma((STREAMS, 13)), dma((STREAMS, 13)),
        ],
        compiler_params=pltpu.CompilerParams(
            collective_id=0, has_side_effects=True, vmem_limit_bytes=67_000_000),
        name="cg_solve",
    )(gram_tiles, right_side)


def solution(mesh):
    return jax.shard_map(
        body,
        mesh=mesh,
        in_specs=(P("rows", "cols"), P(("rows", "cols"), None)),
        out_specs=(P(("rows", "cols"), None), P(("rows", "cols"), None)),
        check_vma=False,
    )
```

time: 522 us -> 245 us (0.47); the launches traced: 513 us -> 244 us
  blocking collectives: 300 us -> 0 us
  Pallas kernels: 0 us -> 240 us
  matrix products: 82.7 us -> 0 us
  local copies, waits for them, and re-layouts: 50.2 us -> 3.09 us
  starting transfers between devices: 29.8 us -> 0 us
  waiting for transfers between devices: 27.7 us -> 0 us
  other arithmetic: 20.9 us -> 0 us
    all_to_all x8 -> x0, blocking collectives: 300 us -> none  [the longest x4 191 us: sent_to_all(): return lax.all_to_all(copies, axis, split_axis=0, concat_axis=0, tiled=True)]
    pallas_call x0 -> x1, Pallas kernels: none -> 240 us  [body(): pl.pallas_call(kernel, out_shape=(shard, shard), in_specs=[pl.BlockSpec(m...]
    dot_general x4 -> x0, matrix products: 82.7 us -> none  [contract(): lax.dot_general(tile_rows, vectors, (((0,), (0,)), ((), ())), precision=l...]
    all_to_all x5 -> x0, starting transfers between devices: 29.8 us -> none  [sent_to_all(): return lax.all_to_all(copies, axis, split_axis=0, concat_axis=0, tiled=True)]
    all_to_all x5 -> x0, waiting for transfers between devices: 27.7 us -> none  [sent_to_all(): return lax.all_to_all(copies, axis, split_axis=0, concat_axis=0, tiled=True)]
    dot_general x2 -> x0, local copies, waits for them, and re-layouts: 23.7 us -> none  [contract(): lax.dot_general(tile_rows, vectors, (((0,), (0,)), ((), ())), precision=l...]
    reshape x9 -> x0, local copies, waits for them, and re-layouts: 18.2 us -> none  [the longest x6 11.5 us: laid_out(): return jnp.moveaxis(pieces, 0, dim).reshape(dims)]
    reduce_sum x12 -> x0, other arithmetic: 10.8 us -> none  [the longest x4 6.26 us: summed_on_arrival(): return jnp.sum(pieces, axis=0)]
  transfers between devices with their start and end apart: 5 -> 0, of which waited for: 5 -> 0; matrix products, arithmetic and copies ran while one was open for 7% -> 0% of each run, Pallas kernels for 0% -> 0%
where the time goes in v1:
time: 245 us; the launch traced here: 244 us
  Pallas kernels  240 us (98%)
  local copies, waits for them, and re-layouts  3.09 us (1%)
    pallas_call x1, Pallas kernels, body(): pl.pallas_call(kernel, out_shape=(shard, shard), in_specs=[pl.BlockSpec(m...  240 us

profile of v1, /device:TPU:8, one launch (start us, length us, event | category | flops | bytes accessed | tf_op | source)
XLA Modules:
  0.0 243.9 jit_solution(15136559649176233515)
XLA Ops:
  0.6 240.1 %cg_solve.1 = (f32[100,256]{1,0:T(8,128)}, f32[100,256]{1,0:T(8,128)}) custom-call(f32[1600,1600]{1,0:T(8,128)} %gram.1, f32[100,256]{1,0:T(8,128)} %rhs.1), custom_call_target="tpu_custom_call" | custom-call | tf_op jit(solution)/shard_map/cg_solve/pallas_call | solution.py:391
  240.8 1.5 copy.6
  242.3 1.5 copy.7

commit v2 on v1

--- a/solution.py
+++ b/solution.py
@@ -1,3 +1,5 @@
+import functools
+
 import jax
 import jax.numpy as jnp
 from jax import lax
@@ -17,7 +19,30 @@
 CHUNK = 4 * SLOT
 F32, BF16 = jnp.float32, jnp.bfloat16
 
-HALF = "g" + "mm" + "g" + "m" + "ggg" + "mm" + "gg" + "m" + "gg" + "mm" + "gg" + "m" + "gggg" + "mm" + "ggg"
+NAMES = ("O0", "O1", "O2", "O3", "O4", "Q0", "Q1", "Q2", "Q3", "Q4")
+HALF = (
+    "m0", "m1", "fx", "Q0", "m2", "n0", "O2", "m3", "n1", "r0", "r1", "Q1", "O3", "O4", "ox", "Q2", "O1",
+    "Q3", "Q4", "up", "..",
+)
+LAST = (
+    "f0",
+    "m0",
+    "m1",
+    "fx",
+    "m2",
+    "n0",
+    "m3",
+    "n1",
+    "r0",
+    "r1",
+    "f1",
+    "ox",
+    "f2",
+    "up",
+)
+LOAD = {1: ["Q0"], 3: ["O2", "Q1"]}
+TURN = {4: ["O1", "O3", "O4"], 7: ["Q2"], 11: ["Q3"]}
+TAIL = ["Q4", ".."]
 
 
 def halves(x):
@@ -26,8 +51,13 @@
     return hi, lo
 
 
-def kernel(gram, rhs, sol, res, tv, tp, t1, t2, tt, vb, ag, os, cr, xa, xs, xb, ys, yr, st, sc, fs, fr,
-           t_sem, y_snd, y_rcv, z_snd, z_rcv, c_snd, c_rcv, xa_snd, xa_rcv, xb_snd, xb_rcv, q_snd, q_rcv,
+def follow(names, steps):
+    for name in names:
+        steps[name]()
+
+
+def kernel(gram, rhs, ox, od, ores, os_, ostep, tv, tp, t1, t2, tt, vb, ag, os, cr, xa, xs, xb, ys, yr, st, sc, fs, fr,
+           t_sem, z_snd, z_rcv, c_snd, c_rcv, xa_snd, xa_rcv, xb_snd, xb_rcv, q_snd, q_rcv,
            f_snd, f_rcv):
     row, col = lax.axis_index("rows"), lax.axis_index("cols")
     xx, yl, core = row // 4, lax.rem(row // 2, 2), lax.rem(row, 2)
@@ -42,7 +72,13 @@
     at_core = (xx * 4 + yl * 2 + 1 - core, col)
     at_yl = (xx * 4 + (1 - yl) * 2 + core, col)
     at_yh = (row, (1 - yh) * NZ + z)
-    partners = [at_core, at_yl, at_yh] + [at_x(d) for d in range(1, NX)] + [at_z(d) for d in range(1, NZ)]
+    at_both = (xx * 4 + (1 - yl) * 2 + 1 - core, col)
+    around = [
+        [at_core, at_yl, at_both],
+        [at_x(d) for d in range(1, NX)] + [at_yh] + [(at_x(d)[0], at_yh[1]) for d in range(1, NX)],
+        [at_z(d) for d in range(1, NZ)],
+    ]
+    partners = around[0] + around[1] + around[2]
 
     def remote(src, dst, snd, rcv, to):
         return pltpu.make_async_remote_copy(
@@ -68,59 +104,72 @@
 
     def gather(t, s):
         par = lax.rem(t, 2)
-        far = ((4, 3), (3, 4))
-
-        def z_copy(kind, way, d):
-            at = slot(kind, -d if way == 0 else d)
-            return remote(ag.at[t, s, at], ag.at[t, s, at], z_snd.at[s, kind, way, d], z_rcv.at[par, s, kind, way, d],
-                          at_z(1 if way == 0 else NZ - 1))
-
-        def z_landing(kind, way, d):
-            at = slot(kind, -d if way == 0 else d)
-            return remote(ag.at[t, s, at], ag.at[t, s, at], z_snd.at[s, kind, way, d - 1],
-                          z_rcv.at[par, s, kind, way, d - 1], at_z(NZ - 1 if way == 0 else 1))
-
-        def y_copy():
-            return remote(ag.at[t, s, slot(0, 0)], ag.at[t, s, slot(0, 0)], y_snd.at[s], y_rcv.at[par, s], at_yh)
-
-        def y_landing():
-            return remote(ag.at[t, s, slot(1, 0)], ag.at[t, s, slot(1, 0)], y_snd.at[s], y_rcv.at[par, s], at_yh)
+        ways = (1, -1)
+
+        def piece(name, way):
+            kind, d = (0 if name[0] == "O" else 1), int(name[1])
+            return ag.at[t, s, slot(kind, -ways[way] * d)]
+
+        def index(name, way):
+            return NAMES.index(name) * 2 + way
+
+        def copy(have, as_name, way, to):
+            src = piece(have, way)
+            k = index(as_name, way)
+            return remote(src, src, z_snd.at[s, k], z_rcv.at[par, s, k], to)
+
+        def landing(name, way):
+            dst = piece(name, way)
+            k = index(name, way)
+            return remote(dst, dst, z_snd.at[s, k], z_rcv.at[par, s, k], at_yh)
+
+        def along(way, hops):
+            return at_z((ways[way] * hops) % NZ)
+
+        def both(have, as_name, hops):
+            return [copy(have, as_name, way, along(way, hops)) for way in range(2)]
+
+        def begin():
+            return [copy("O0", "Q0", 0, at_yh)] + both("O0", "O2", 2) + both("O0", "O1", 1)
+
+        sends = lambda: {
+            "Q0": [both("Q0", "Q1", 1), []],
+            "Q1": [[copy("Q1", "Q2", 0, along(0, 1))], [copy("Q1", "Q2", 1, along(1, 1))]],
+            "O2": [[copy("O2", "O3", 0, along(0, 1)), copy("O2", "O4", 0, along(0, 2))],
+                   [copy("O2", "O3", 1, along(1, 1))]],
+            "O3": [[copy("O3", "Q3", 0, at_yh)], [copy("O3", "Q3", 1, at_yh)]],
+            "O4": [[copy("O4", "Q4", 0, at_yh)]],
+        }
 
         def first():
-            y_copy().start()
-            z_copy(0, 0, 0).start()
-            z_copy(0, 1, 0).start()
+            for c in begin():
+                c.start()
             pack(t, s, slot(0, 0))
 
-        def other():
-            y_landing().wait_recv()
-            z_copy(1, 0, 0).start()
-            z_copy(1, 1, 0).start()
-            pack(t, s, slot(1, 0))
-
-        def step(kind, d):
+        def take(name, count=2):
             def run():
-                for way in range(2):
-                    if d <= far[kind][way]:
-                        z_landing(kind, way, d).wait_recv()
-                        if d < far[kind][way]:
-                            z_copy(kind, way, d).start()
-                for way in range(2):
-                    if d <= far[kind][way]:
-                        pack(t, s, slot(kind, -d if way == 0 else d))
+                onward = sends().get(name, [[], []])
+                for way in range(count):
+                    landing(name, way).wait_recv()
+                    for c in onward[way]:
+                        c.start()
+                for way in range(count):
+                    kind, d = (0 if name[0] == "O" else 1), int(name[1])
+                    pack(t, s, slot(kind, -ways[way] * d))
             return run
 
         def drain():
-            y_copy().wait_send()
-            for kind in range(2):
-                for way in range(2):
-                    for d in range(far[kind][way]):
-                        z_copy(kind, way, d).wait_send()
-
-        return [first, step(0, 1), other, step(0, 2), step(1, 1), step(0, 3), step(1, 2), step(0, 4), step(1, 3),
-                step(1, 4), drain]
-
-    def scatter(t, s):
+            for c in begin():
+                c.wait_send()
+            for group in sends().values():
+                for some in group:
+                    for c in some:
+                        c.wait_send()
+
+        return first, {"Q0": take("Q0", 1), "O2": take("O2"), "Q1": take("Q1"), "O1": take("O1"), "O3": take("O3"),
+                       "O4": take("O4", 1), "Q2": take("Q2"), "Q3": take("Q3"), "Q4": take("Q4", 1), "..": drain}
+
+    def scatter(t, s, start_next=True):
         par = lax.rem(t, 2)
         ahead = (2, 1, 3, 0)
 
@@ -213,10 +262,12 @@
 
         def last():
             update()
+            if start_next:
+                pl.when(t < ITERS - 1)(gather(t + 1, s)[0])
             drain()
 
-        return [multiply(0), multiply(1), far_x, multiply(2), near_x(0), multiply(3), near_x(1), relay_x(0), relay_x(1),
-                own_x, last]
+        return {"m0": multiply(0), "m1": multiply(1), "m2": multiply(2), "m3": multiply(3), "fx": far_x,
+                "n0": near_x(0), "n1": near_x(1), "r0": relay_x(0), "r1": relay_x(1), "ox": own_x, "up": last}
 
     R, W, Z, S, D, X = range(6)
 
@@ -270,8 +321,10 @@
         ag[t + 1, s, mine, 102:104] = jnp.zeros((2, NC), F32)
 
     def finish(s):
-        plan = [[(at_core, 0)], [(at_yl, 1)], [(at_x(d), 1 + d) for d in range(1, NX)], [(at_yh, 5)],
-                [(at_z(d), 5 + d) for d in range(1, NZ)]]
+        plan, first = [], 0
+        for group in around:
+            plan.append([(to, first + k) for k, to in enumerate(group)])
+            first += len(group)
 
         def copies(stage):
             return [remote(fs.at[s, stage], fr.at[s, k], f_snd.at[s, k], f_rcv.at[s, k], to) for to, k in plan[stage]]
@@ -309,13 +362,17 @@
             ss = w + beta * st[s, S, 0:PIECE]
             dd = r + beta * st[s, D, 0:PIECE]
             cols = slice(s * NC, (s + 1) * NC)
-            sol[:, cols] = st[s, X, 0:PIECE] + step * dd
-            res[:, cols] = r - step * ss
+            ox[:, cols] = st[s, X, 0:PIECE]
+            od[:, cols] = dd
+            ores[:, cols] = r
+            os_[:, cols] = ss
+            ostep[:, cols] = jnp.broadcast_to(step, (8, NC))
             for stage in range(len(plan)):
                 for c in copies(stage):
                     c.wait_send()
 
-        return [begin] + [onward(k) for k in range(1, len(plan))] + [close]
+        steps = [begin] + [onward(k) for k in range(1, len(plan))] + [close]
+        return {"f%d" % i: run for i, run in enumerate(steps)}
 
     mine = slot(0, 0)
     st[...] = jnp.zeros(st.shape, F32)
@@ -328,9 +385,8 @@
     for a in range(16):
         t2[a * SLOT + PIECE:(a + 1) * SLOT] = jnp.zeros((SLOT - PIECE, 128), F32)
     pl.semaphore_wait(barrier, len(partners))
-    events = gather(0, 0)
-    events[0]()
-    events = events[1:]
+    begin, events = gather(0, 0)
+    begin()
 
     @pl.loop(0, 4)
     def _(m):
@@ -344,6 +400,8 @@
                 v = tv[pl.ds(base, 200), lane:lane + wide]
                 none = jnp.zeros((KSLOT - PIECE, wide), F32)
                 tp[pl.ds(into, 224), lane:lane + wide] = jnp.concatenate([v[0:100], none, v[100:200], none], axis=0)
+        for when, names in LOAD.items():
+            pl.when(m == when)(functools.partial(follow, names, events))
 
 
     @pl.loop(0, KPAD // 128)
@@ -359,28 +417,24 @@
             start = (p % 2) * 208
             tt[p // 2, start:start + 208, pl.ds(at, 128)] = hi
             tt[p // 2, CHUNK + start:CHUNK + start + 208, pl.ds(at, 128)] = lo
-        for i, event in enumerate(events):
-            pl.when(kb == 4 + i)(event)
-
-    def interleave(plan, g, m):
-        g, m = list(g), list(m)
-        for what in plan:
-            if what == "g" and g:
-                g.pop(0)()
-            if what == "m" and m:
-                m.pop(0)()
-        for run in m + g:
-            run()
+        for when, names in TURN.items():
+            pl.when(kb == when)(functools.partial(follow, names, events))
+
+    gather(0, 1)[0]()
+    follow(TAIL, events)
 
     @pl.loop(0, STREAMS * ITERS - 1)
     def _(h):
         sm, tm = lax.rem(h, 2), h // 2
         sg, tg = 1 - sm, (h + 1) // 2
-        interleave(HALF, gather(tg, sg), scatter(tm, sm))
-
-    interleave("gm" + "mmg" + "mmg" + "mmmg" + "mg" + "mg" + "mg", finish(0), scatter(ITERS - 1, 1))
-    for run in finish(1):
-        run()
+        follow(HALF, gather(tg, sg)[1] | scatter(tm, sm))
+
+    ending = finish(0)
+    follow(LAST, ending | scatter(ITERS - 1, 1, False))
+    other = finish(1)
+    follow(["f0"], other)
+    follow(["f3"], ending)
+    follow(["f1", "f2", "f3"], other)
 
 
 def body(gram_tiles, right_side):
@@ -388,11 +442,11 @@
     dma = pltpu.SemaphoreType.DMA
     vmem = pltpu.VMEM
     spec = pl.BlockSpec(memory_space=pltpu.VMEM)
-    return pl.pallas_call(
+    x, d, r, s, step = pl.pallas_call(
         kernel,
-        out_shape=(shard, shard),
+        out_shape=(shard,) * 4 + (jax.ShapeDtypeStruct((8, right_side.shape[1]), F32),),
         in_specs=[pl.BlockSpec(memory_space=pl.ANY), spec],
-        out_specs=(spec, spec),
+        out_specs=(spec,) * 5,
         scratch_shapes=[
             vmem((ROWS, ROWS), F32),
             vmem((KPAD, ROWS), F32),
@@ -410,21 +464,22 @@
             vmem((ITERS, STREAMS, SLOT, NC), F32),
             vmem((STREAMS, 6, SLOT, NC), F32),
             vmem((STREAMS, 8, NC), F32),
-            vmem((STREAMS, 5, 8, NC), F32),
-            vmem((STREAMS, 13, 8, NC), F32),
+            vmem((STREAMS, 3, 8, NC), F32),
+            vmem((STREAMS, 17, 8, NC), F32),
             dma((4,)),
-            dma((STREAMS,)), dma((2, STREAMS)),
-            dma((STREAMS, 2, 2, 4)), dma((2, STREAMS, 2, 2, 4)),
+            dma((STREAMS, 20)), dma((2, STREAMS, 20)),
             dma((STREAMS, 4)), dma((2, STREAMS, 4)),
             dma((STREAMS, 2)), dma((2, STREAMS, 2)),
             dma((STREAMS, 2, 2)), dma((2, STREAMS, 2, 2)),
             dma((STREAMS,)), dma((2, STREAMS)),
-            dma((STREAMS, 13)), dma((STREAMS, 13)),
+            dma((STREAMS, 17)), dma((STREAMS, 17)),
         ],
         compiler_params=pltpu.CompilerParams(
             collective_id=0, has_side_effects=True, vmem_limit_bytes=67_000_000),
         name="cg_solve",
     )(gram_tiles, right_side)
+    step = step[0:1]
+    return x + step * d, r - step * s
 
 
 def solution(mesh):

time: 245 us -> 170 us (0.69)
  Pallas kernels: 240 us -> 166 us
    pallas_call x1, Pallas kernels: 240 us -> 166 us  [body(): pl.pallas_call(kernel, out_shape=(shard,) * 4 + (jax.ShapeDtypeStruct((8,...]
    unnamed x2 -> x0, local copies, waits for them, and re-layouts: 3.09 us -> none
where the time goes in v2:
time: 170 us
  Pallas kernels  166 us (98%)
  other arithmetic  1.75 us (1%)
    pallas_call x1, Pallas kernels, body(): pl.pallas_call(kernel, out_shape=(shard,) * 4 + (jax.ShapeDtypeStruct((8,...  166 us

profile of v2, /device:TPU:8, one launch (start us, length us, event | category | flops | bytes accessed | tf_op | source)
XLA Modules:
  0.0 169.6 jit_solution(11780738534238199944)
XLA Ops:
  0.6 166.5 %cg_solve.1 = (f32[100,256]{1,0:T(8,128)}, f32[100,256]{1,0:T(8,128)}, f32[100,256]{1,0:T(8,128)}, f32[100,256]{1,0:T(8,128)}, f32[8,256]{1,0:T(8,128)}) custom-call(f32[1600,1600]{1,0:T(8,128)} %gram.1, f32[100,256]{1,0:T(8,128)} %rhs.1), custom_call_target="tpu_custom_call" | custom-call | tf_op jit(solution)/shard_map/cg_solve/pallas_call | solution.py:445
  167.1 0.7 slice.3
  167.8 1.8 %multiply_subtract_fusion = (f32[100,256]{1,0:T(8,128)}, f32[100,256]{1,0:T(8,128)}) fusion(f32[100,256]{1,0:T(8,128)} %get-tuple-element.10, f32[100,256]{1,0:T(8,128)} %get-tuple-element.11, f32[256]{0:T(256)S(1)} %bitcast.1, f32[100,256]{1,0:T(8,128)} %get-tuple-element.7, f32[100,256]{1,0:T(8,128)} %get-tuple-element.9), kind=kLoop, calls=%fused_computation | loop fusion | flops 102400 | bytes 615424 | tf_op jit(solution)/shard_map/sub | solution.py:482

commit v3 on v2

--- a/solution.py
+++ b/solution.py
@@ -21,8 +21,27 @@
 
 NAMES = ("O0", "O1", "O2", "O3", "O4", "Q0", "Q1", "Q2", "Q3", "Q4")
 HALF = (
-    "m0", "m1", "fx", "Q0", "m2", "n0", "O2", "m3", "n1", "r0", "r1", "Q1", "O3", "O4", "ox", "Q2", "O1",
-    "Q3", "Q4", "up", "..",
+    "m0",
+    "m1",
+    "fx",
+    "Q0",
+    "m2",
+    "n0",
+    "O2",
+    "m3",
+    "n1",
+    "r0",
+    "r1",
+    "O3",
+    "O4",
+    "ox",
+    "Q1",
+    "Q2",
+    "O1",
+    "Q3",
+    "Q4",
+    "up",
+    "..",
 )
 LAST = (
     "f0",
@@ -110,16 +129,20 @@
             kind, d = (0 if name[0] == "O" else 1), int(name[1])
             return ag.at[t, s, slot(kind, -ways[way] * d)]
 
+        def view(have, way, name):
+            src = piece(have, way)
+            return src.at[(pl.ds(0, 56), pl.ds(56, 48))[way]] if name[1] == "4" else src
+
         def index(name, way):
             return NAMES.index(name) * 2 + way
 
         def copy(have, as_name, way, to):
-            src = piece(have, way)
+            src = view(have, way, as_name)
             k = index(as_name, way)
             return remote(src, src, z_snd.at[s, k], z_rcv.at[par, s, k], to)
 
         def landing(name, way):
-            dst = piece(name, way)
+            dst = view(name, way, name)
             k = index(name, way)
             return remote(dst, dst, z_snd.at[s, k], z_rcv.at[par, s, k], at_yh)
 
@@ -134,11 +157,10 @@
 
         sends = lambda: {
             "Q0": [both("Q0", "Q1", 1), []],
-            "Q1": [[copy("Q1", "Q2", 0, along(0, 1))], [copy("Q1", "Q2", 1, along(1, 1))]],
-            "O2": [[copy("O2", "O3", 0, along(0, 1)), copy("O2", "O4", 0, along(0, 2))],
-                   [copy("O2", "O3", 1, along(1, 1))]],
+            "O2": [[copy("O2", "O3", way, along(way, 1)), copy("O2", "O4", way, along(way, 2)),
+                    copy("O2", "Q2", way, at_yh)] for way in range(2)],
             "O3": [[copy("O3", "Q3", 0, at_yh)], [copy("O3", "Q3", 1, at_yh)]],
-            "O4": [[copy("O4", "Q4", 0, at_yh)]],
+            "O4": [[copy("O4", "Q4", way, at_yh)] for way in range(2)],
         }
 
         def first():
@@ -153,7 +175,7 @@
                     landing(name, way).wait_recv()
                     for c in onward[way]:
                         c.start()
-                for way in range(count):
+                for way in range(1 if name[1] == "4" else count):
                     kind, d = (0 if name[0] == "O" else 1), int(name[1])
                     pack(t, s, slot(kind, -ways[way] * d))
             return run
@@ -167,7 +189,7 @@
                         c.wait_send()
 
         return first, {"Q0": take("Q0", 1), "O2": take("O2"), "Q1": take("Q1"), "O1": take("O1"), "O3": take("O3"),
-                       "O4": take("O4", 1), "Q2": take("Q2"), "Q3": take("Q3"), "Q4": take("Q4", 1), "..": drain}
+                       "O4": take("O4"), "Q2": take("Q2"), "Q3": take("Q3"), "Q4": take("Q4"), "..": drain}
 
     def scatter(t, s, start_next=True):
         par = lax.rem(t, 2)
@@ -417,10 +439,10 @@
             start = (p % 2) * 208
             tt[p // 2, start:start + 208, pl.ds(at, 128)] = hi
             tt[p // 2, CHUNK + start:CHUNK + start + 208, pl.ds(at, 128)] = lo
+        pl.when(kb == 8)(gather(0, 1)[0])
         for when, names in TURN.items():
             pl.when(kb == when)(functools.partial(follow, names, events))
 
-    gather(0, 1)[0]()
     follow(TAIL, events)
 
     @pl.loop(0, STREAMS * ITERS - 1)

time: 170 us -> 164 us (0.965)
  Pallas kernels: 166 us -> 161 us
    pallas_call x1, Pallas kernels: 166 us -> 161 us  [body(): pl.pallas_call(kernel, out_shape=(shard,) * 4 + (jax.ShapeDtypeStruct((8,...]
where the time goes in v3:
time: 164 us
  Pallas kernels  161 us (98%)
  other arithmetic  1.75 us (1%)
    pallas_call x1, Pallas kernels, body(): pl.pallas_call(kernel, out_shape=(shard,) * 4 + (jax.ShapeDtypeStruct((8,...  161 us

profile of v3, /device:TPU:8, one launch (start us, length us, event | category | flops | bytes accessed | tf_op | source)
XLA Modules:
  0.0 164.0 jit_solution(4861732619628630365)
XLA Ops:
  0.6 160.9 %cg_solve.1 = (f32[100,256]{1,0:T(8,128)}, f32[100,256]{1,0:T(8,128)}, f32[100,256]{1,0:T(8,128)}, f32[100,256]{1,0:T(8,128)}, f32[8,256]{1,0:T(8,128)}) custom-call(f32[1600,1600]{1,0:T(8,128)} %gram.1, f32[100,256]{1,0:T(8,128)} %rhs.1), custom_call_target="tpu_custom_call" | custom-call | tf_op jit(solution)/shard_map/cg_solve/pallas_call | solution.py:467
  161.6 0.7 slice.3
  162.3 1.8 %multiply_subtract_fusion = (f32[100,256]{1,0:T(8,128)}, f32[100,256]{1,0:T(8,128)}) fusion(f32[100,256]{1,0:T(8,128)} %get-tuple-element.10, f32[100,256]{1,0:T(8,128)} %get-tuple-element.11, f32[256]{0:T(256)S(1)} %bitcast.1, f32[100,256]{1,0:T(8,128)} %get-tuple-element.7, f32[100,256]{1,0:T(8,128)} %get-tuple-element.9), kind=kLoop, calls=%fused_computation | loop fusion | flops 102400 | bytes 615424 | tf_op jit(solution)/shard_map/sub | solution.py:504
